TPU v7x, 32 devices: a whole 2x2x4 slice. The times are simulated.
32 devices in a mesh: row: 4 (over y, core), col: 8 (over z, x).
Axes of the slice: x: 2, y: 2, z: 4, core: 2. Of those that a mesh axis runs over, the one named last changes fastest.
Arguments:
- ainv_top: float32 [4096, 4096], P('row', 'col'), may hold values from -0.25 to 0.25
- par_struct: int32 [8, 16], replicated, may hold values from 0 to 31, as said below
- par_panel: float32 [8, 16, 128, 128], P('col', 'row'), may hold values from -6 to 6
- par_linv: float32 [8, 128, 128], P('col', 'row'), may hold values from -0.0625 to 0.0625
- par_dinv: float32 [8, 128, 128], P('col', 'row'), may hold values from -192 to 192
- kid_panel: float32 [16, 16, 128, 128], P('col', 'row'), may hold values from -6 to 6
- kid_upper: float32 [16, 128, 128], P('col', 'row'), may hold values from -6 to 6
- kid_linv: float32 [16, 128, 128], P('col', 'row'), may hold values from -0.0625 to 0.0625
- kid_dinv: float32 [16, 128, 128], P('col', 'row'), may hold values from -192 to 192
Outputs:
- par_offdiag: float32 [8, 16, 128, 128], P('col', 'row')
- par_diag: float32 [8, 128, 128], P('col', 'row')
- kid_offdiag: float32 [16, 16, 128, 128], P('col', 'row')
- kid_parent: float32 [16, 128, 128], P('col', 'row')
- kid_diag: float32 [16, 128, 128], P('col', 'row')
Inputs may be any that keep to these rules, and one draw needn't show every extreme that they name: `par_struct`: in every row, entries 2j and 2j + 1 are two different ancestors among j * 4 to (j + 1) * 4 - 1.
All inputs are finite; a program needn't handle non-finite values.
Results may differ from a plain program's by a relative error of at most 0.00014.
Values sent between devices are 32-bit elements; how exact they have to be, the bound alone decides.
No kernel may reach another device: no remote copies, remote signals or barrier semaphores. Data moves between devices by JAX's collectives and lax.ppermute only.
A program may use at most 128 MiB of HBM per device.

v0:
```python
import jax
import jax.numpy as jnp
from jax import lax
from jax.sharding import PartitionSpec as P

high = lax.Precision.HIGH
highest = lax.Precision.HIGHEST


def mm(spec, *operands, precision=high):
    return jnp.einsum(spec, *operands, precision=precision)


def on_device(
    ainv_top, par_struct, par_panel, par_linv, par_dinv, kid_panel, kid_upper, kid_linv, kid_dinv
):
    grid_rows = lax.axis_size("row")
    grid_cols = lax.axis_size("col")
    my_row = lax.axis_index("row")
    my_col = lax.axis_index("col")
    width = par_panel.shape[-1]
    band_rows = width // grid_rows
    slot_share = par_panel.shape[1]
    children = kid_panel.shape[0]
    pair_width = par_struct.shape[1] // grid_cols
    tile_rows = ainv_top.shape[0] // width
    tile_cols = ainv_top.shape[1] // width
    local_tiles = ainv_top.reshape(tile_rows, width, tile_cols, width)
    pick_rows = lax.dynamic_slice_in_dim(par_struct, my_row * slot_share, slot_share, 1)
    pick_cols = lax.dynamic_slice_in_dim(par_struct, my_col * pair_width, pair_width, 1)
    pick_rows = pick_rows - my_row * tile_rows
    pick_cols = pick_cols - my_col * tile_cols
    tiles = local_tiles[pick_rows[:, :, None], :, pick_cols[:, None, :], :]
    small = jnp.concatenate([par_linv, par_dinv, kid_upper, kid_linv, kid_dinv], axis=0)
    small = lax.all_gather(small, "row", axis=1, tiled=True)
    plinv, pdinv = (small[0], small[1])
    kupper = small[2 : 2 + children]
    klinv = small[2 + children : 2 + 2 * children]
    kdinv = small[2 + 2 * children :]
    panels = jnp.concatenate([par_panel, kid_panel], axis=0)
    every = lax.all_gather(panels, "row", axis=1, tiled=True)
    moved = lax.all_to_all(tiles, "col", 0, 0, tiled=True)
    every = every.reshape(1 + children, grid_cols, pair_width, width, width)
    prod = mm("cjkab,nckbd->njad", moved, every)
    par_off = -mm("jab,bc->jac", prod[0], plinv)
    par_hat = mm("jab,bc->jac", par_panel[0], plinv)
    kid_hat = mm("njab,nbc->njac", kid_panel, klinv)
    kuphat = mm("nab,nbc->nac", kupper, klinv)
    kid_sum = prod[1:] + mm("jab,nbc->njac", par_off, kupper)
    kid_off = -mm("njab,nbc->njac", kid_sum, klinv)
    diag_part = mm("jba,jbc->ac", par_hat, par_off)
    parent_part = mm("jba,njbc->nac", par_off, kid_hat)
    hat_part = mm("njba,njbc->nac", kid_hat, kid_off)
    inner = parent_part - mm("ab,nbc->nac", diag_part, kuphat)
    edge_part = mm("nba,nbc->nac", kuphat, inner) - hat_part
    parts = jnp.concatenate([diag_part[None], parent_part, edge_part], axis=0)
    parts = parts.reshape(1 + 2 * children, grid_rows, band_rows, width)
    parts = lax.all_to_all(parts, "row", 1, 1, tiled=True)
    sums = parts.sum(axis=1)
    par_pivot = mm("ba,bc,cd->ad", plinv, pdinv, plinv)
    kid_pivot = mm("nba,nbc,ncd->nad", klinv, kdinv, klinv)
    kid_pivot = kid_pivot + mm("nba,bc,ncd->nad", kuphat, par_pivot, kuphat)
    start = my_row * band_rows
    par_diag = lax.dynamic_slice_in_dim(par_pivot, start, band_rows, 0) - sums[0]
    kid_par = -(sums[1 : 1 + children] + mm("ab,nbc->nac", par_diag, kuphat))
    kid_diag = lax.dynamic_slice_in_dim(kid_pivot, start, band_rows, 1) + sums[1 + children :]
    return (par_off[None], par_diag[None], kid_off, kid_par, kid_diag)


def solution(mesh):
    placed = (
        P("row", "col"),
        P(),
        P("col", "row", None, None),
        P("col", "row", None),
        P("col", "row", None),
        P("col", "row", None, None),
        P("col", "row", None),
        P("col", "row", None),
        P("col", "row", None),
    )
    return jax.shard_map(
        on_device,
        mesh=mesh,
        in_specs=placed,
        out_specs=(
            P("col", "row", None, None),
            P("col", "row", None),
            P("col", "row", None, None),
            P("col", "row", None),
            P("col", "row", None),
        ),
        check_vma=False,
    )
```

profile of v0, /device:TPU:0, one launch (start us, length us, event | category | flops | bytes accessed | tf_op | source)
XLA Modules:
  0.0 147.9 jit_solution(1128994719983951276)
XLA Ops:
  7.2 0.8 fusion.41
  7.9 0.8 fusion.43
  8.9 2.9 %reshape.58 = f32[8,128,4,128]{3,2,1,0:T(4,128)} reshape(f32[1024,512]{1,0:T(8,128)} %param.9) | data formatting | bytes 4194304 | tf_op jit(solution)/shard_map/reshape | solution.py:28
  11.8 1.9 %copy.49 = f32[8,128,4,128]{3,1,2,0:T(8,128)S(1)} copy(f32[8,128,4,128]{3,2,1,0:T(4,128)} %reshape.58) | data formatting | bytes 4194304 | tf_op jit(solution)/shard_map/reshape | solution.py:28
  13.7 2.9 %gather_fusion = f32[64,128,128]{2,1,0:T(8,128)} fusion(f32[8,128,4,128]{3,1,2,0:T(8,128)S(1)} %copy.49, s32[64]{0:T(128)S(1)} %reshape.36), kind=kCustom, calls=%fused_computation | custom fusion | bytes 8389120 | tf_op jit(solution)/shard_map/gather | solution.py:33
  16.6 7.4 %all-to-all-start = ((f32[8,4,2,128,128]{4,3,2,1,0:T(8,128)}), f32[8,4,2,128,128]{4,3,2,1,0:T(8,128)}, u32[]{:S(2)}, u32[]{:S(2)}) async-start(f32[8,4,2,128,128]{4,3,2,1,0:T(8,128)} %bitcast.134), calls=%async_computation | async-start | bytes 8388608 | tf_op jit(solution)/shard_map/all_to_all | solution.py:42
  24.0 1.0 pad_maximum_fusion
  25.1 7.2 %all_gather.7 = f32[8,128,128]{2,1,0:T(8,128)S(1)} all-gather(f32[8,32,128]{2,1,0:T(8,128)S(1)} %constant_dynamic-update-slice_fusion), channel_id=1, replica_groups=mesh['row'=4,'col'=8] {'row'}, dimensions={1}, use_global_device_ids=true | all-gather | bytes 655360 | tf_op jit(solution)/shard_map/all_gather | solution.py:35
  32.3 0.3 fusion.24
  32.6 0.2 fusion.30
  32.8 0.2 fusion.21
  33.0 0.3 fusion.25
  33.3 0.3 convolution_bitcast_fusion.2
  33.7 0.3 fusion.17
  34.0 0.4 convolution_bitcast_fusion.1
  34.4 22.1 %all-gather.2.cloned.1.call-done = f32[3,16,128,128]{3,2,1,0:T(8,128)} async-done(((f32[3,4,128,128]{3,2,1,0:T(8,128)}), f32[3,16,128,128]{3,2,1,0:T(8,128)}) %all-gather.2.cloned.1.call-update) | async-done | bytes 3145744 | tf_op jit(solution)/shard_map/all_gather | solution.py:41
  56.5 60.8 %all-to-all-done = f32[8,4,2,128,128]{4,3,2,1,0:T(8,128)} async-done(((f32[8,4,2,128,128]{4,3,2,1,0:T(8,128)}), f32[8,4,2,128,128]{4,3,2,1,0:T(8,128)}, u32[]{:S(2)}, u32[]{:S(2)}) %all-to-all-start) | async-done | bytes 4194336 | tf_op jit(solution)/shard_map/all_to_all | solution.py:42
  117.3 7.8 %fusion.3 = f32[3,4,128,128]{2,3,1,0:T(8,128)S(1)} fusion(f32[3,8,2,128,128,1]{4,3,2,1,5,0:T(8,128)} %bitcast.136, f32[8,4,2,128,128]{4,3,2,1,0:T(8,128)} %all-to-all-done), kind=kOutput, calls=%fused_computation.4 | convolution fusion | flops 2415919104 | bytes 8126464 | tf_op jit(solution)/shard_map/cjkab,nckbd->njad/dot_general | solution.py:11
  125.1 0.4 convolution_negate_fusion.1
  125.5 0.4 fusion.6
  126.0 0.4 fusion.11
  126.3 0.3 fusion.45
  126.6 0.6 convolution_negate_fusion
  127.2 0.4 convolution_bitcast_fusion.3
  127.6 0.2 fusion.7
  127.8 0.3 convolution_subtract_fusion
  128.1 0.7 pad_maximum_fusion.1
  128.8 3.5 %all-to-all-start.1 = ((f32[5,4,32,128]{3,2,0,1:T(8,128)}), f32[5,4,32,128]{3,2,0,1:T(8,128)S(1)}, u32[]{:S(2)}, u32[]{:S(2)}) async-start(f32[5,4,32,128]{3,2,0,1:T(8,128)} %pad_maximum_fusion.1), calls=%async_computation.1 | async-start | bytes 655360 | tf_op jit(solution)/shard_map/all_to_all | solution.py:58
  132.7 6.3 %all-to-all-done.1 = f32[5,4,32,128]{3,2,0,1:T(8,128)S(1)} async-done(((f32[5,4,32,128]{3,2,0,1:T(8,128)}), f32[5,4,32,128]{3,2,0,1:T(8,128)S(1)}, u32[]{:S(2)}, u32[]{:S(2)}) %all-to-all-start.1) | async-done | bytes 327712 | tf_op jit(solution)/shard_map/all_to_all | solution.py:58
  139.0 0.8 fusion.9
  139.8 0.6 fusion.39
  140.4 0.6 slice_add_fusion
  (30 shorter events, 0.7 us)
Async XLA Ops:
  16.5 7.5 %copy-start.1 = (f32[2,4,128,128]{3,2,1,0:T(8,128)S(1)}, f32[2,4,128,128]{3,2,1,0:T(8,128)}, u32[]{:S(2)}) copy-start(f32[2,4,128,128]{3,2,1,0:T(8,128)} %param.14) | copy-start | bytes 1572868
  16.5 7.5 %copy-start.3 = (f32[1,4,128,128]{3,2,1,0:T(8,128)S(1)}, f32[1,4,128,128]{3,2,1,0:T(8,128)}, u32[]{:S(2)}) copy-start(f32[1,4,128,128]{3,2,1,0:T(8,128)} %param.11) | copy-start | bytes 786436
  16.5 8.5 %copy-start.7 = (f32[1,32,128]{2,1,0:T(8,128)S(1)}, f32[1,32,128]{2,1,0:T(8,128)}, u32[]{:S(2)}) copy-start(f32[1,32,128]{2,1,0:T(8,128)} %param.12) | copy-start | bytes 49156
  16.5 8.5 %copy-start.8 = (f32[1,32,128]{2,1,0:T(8,128)S(1)}, f32[1,32,128]{2,1,0:T(8,128)}, u32[]{:S(2)}) copy-start(f32[1,32,128]{2,1,0:T(8,128)} %param.13) | copy-start | bytes 49156
  16.5 8.5 %copy-start.4 = (f32[2,32,128]{2,1,0:T(8,128)S(1)}, f32[2,32,128]{2,1,0:T(8,128)}, u32[]{:S(2)}) copy-start(f32[2,32,128]{2,1,0:T(8,128)} %param.15) | copy-start | bytes 98308
  16.6 8.5 %copy-start.5 = (f32[2,32,128]{2,1,0:T(8,128)S(1)}, f32[2,32,128]{2,1,0:T(8,128)}, u32[]{:S(2)}) copy-start(f32[2,32,128]{2,1,0:T(8,128)} %param.16) | copy-start | bytes 98308
  16.6 8.5 %copy-start.6 = (f32[2,32,128]{2,1,0:T(8,128)S(1)}, f32[2,32,128]{2,1,0:T(8,128)}, u32[]{:S(2)}) copy-start(f32[2,32,128]{2,1,0:T(8,128)} %param.17) | copy-start | bytes 98308
  16.6 100.7 %all-to-all-start = ((f32[8,4,2,128,128]{4,3,2,1,0:T(8,128)}), f32[8,4,2,128,128]{4,3,2,1,0:T(8,128)}, u32[]{:S(2)}, u32[]{:S(2)}) async-start(f32[8,4,2,128,128]{4,3,2,1,0:T(8,128)} %bitcast.134), calls=%async_computation | async-start | bytes 8388608 | tf_op jit(solution)/shard_map/all_to_all | solution.py:42
  24.0 32.5 %all-gather.2.cloned.1.call-start = ((), (), s32[]{:S(2)}) async-start(), calls=%async_computation.2 | async-start | bytes 3932160 | tf_op jit(solution)/shard_map/all_gather | solution.py:41
  125.5 7.2 %copy-start = (f32[4,128,128]{2,1,0:T(8,128)}, f32[4,128,128]{2,1,0:T(8,128)S(1)}, u32[]{:S(2)}) copy-start(f32[4,128,128]{2,1,0:T(8,128)S(1)} %convolution_negate_fusion.1) | copy-start | bytes 786436
  127.2 13.8 %copy-start.2 = (f32[2,4,128,128]{3,2,1,0:T(8,128)}, f32[2,4,128,128]{3,2,1,0:T(8,128)S(1)}, u32[]{:S(2)}) copy-start(f32[2,4,128,128]{3,2,1,0:T(8,128)S(1)} %convolution_negate_fusion) | copy-start | bytes 1572868
  128.8 10.2 %all-to-all-start.1 = ((f32[5,4,32,128]{3,2,0,1:T(8,128)}), f32[5,4,32,128]{3,2,0,1:T(8,128)S(1)}, u32[]{:S(2)}, u32[]{:S(2)}) async-start(f32[5,4,32,128]{3,2,0,1:T(8,128)} %pad_maximum_fusion.1), calls=%async_computation.1 | async-start | bytes 655360 | tf_op jit(solution)/shard_map/all_to_all | solution.py:58
Sparse Core Ops, SparseCore 0:
  26.4 30.0 all-gather.1
where the time goes:
time: 148 us
  waiting for transfers between devices  89.2 us (60%)
  between operations  14.3 us (10%)
  matrix products  13.9 us (9%)
  starting transfers between devices  10.9 us (7%)
  local copies, waits for them, and re-layouts  7.82 us (5%)
  blocking collectives  7.2 us (5%)
  other arithmetic  4.55 us (3%)
    all_to_all x1, waiting for transfers between devices, on_device(): moved = lax.all_to_all(tiles, 'col', 0, 0, tiled=True)  60.8 us
    all_gather x1, waiting for transfers between devices, on_device(): every = lax.all_gather(panels, 'row', axis=1, tiled=True)  22.1 us
    dot_general x19, matrix products, mm(): return jnp.einsum(spec, *operands, precision=precision)  13.9 us
    all_to_all x1, starting transfers between devices, on_device(): moved = lax.all_to_all(tiles, 'col', 0, 0, tiled=True)  7.4 us
    all_gather x1, blocking collectives, on_device(): small = lax.all_gather(small, 'row', axis=1, tiled=True)  7.2 us
    all_to_all x1, waiting for transfers between devices, on_device(): parts = lax.all_to_all(parts, 'row', 1, 1, tiled=True)  6.27 us
    reshape x2, local copies, waits for them, and re-layouts, on_device(): local_tiles = ainv_top.reshape(tile_rows, width, tile_cols, width)  4.78 us
    all_to_all x1, starting transfers between devices, on_device(): parts = lax.all_to_all(parts, 'row', 1, 1, tiled=True)  3.45 us
  transfers between devices with their start and end apart: 3, of which 3 were waited for; matrix products, arithmetic and copies ran while one was open for 2% of the time, Pallas kernels for 0%

commit v1 on v0

--- a/solution.py
+++ b/solution.py
@@ -38,7 +38,16 @@
     klinv = small[2 + children : 2 + 2 * children]
     kdinv = small[2 + 2 * children :]
     panels = jnp.concatenate([par_panel, kid_panel], axis=0)
-    every = lax.all_gather(panels, "row", axis=1, tiled=True)
+    ways = lax.axis_size("row")
+    up = [(d, (d + 1) % ways) for d in range(ways)]
+    down = [(d, (d - 1) % ways) for d in range(ways)]
+    earlier, later = ([panels], [panels])
+    for _ in range(ways // 2):
+        earlier.append(lax.ppermute(earlier[-1], "row", up))
+    for _ in range((ways - 1) // 2):
+        later.append(lax.ppermute(later[-1], "row", down))
+    line = jnp.concatenate([*earlier[::-1], *later[1:]], axis=1)
+    every = jnp.roll(line, (lax.axis_index("row") - ways // 2) * panels.shape[1], axis=1)
     moved = lax.all_to_all(tiles, "col", 0, 0, tiled=True)
     every = every.reshape(1 + children, grid_cols, pair_width, width, width)
     prod = mm("cjkab,nckbd->njad", moved, every)

time: 148 us -> 133 us (0.90)
  waiting for transfers between devices: 89.2 us -> 65.8 us
  blocking collectives: 7.2 us -> 21.9 us
  between operations: 14.3 us -> 1.08 us
  local copies, waits for them, and re-layouts: 7.82 us -> 12.3 us
  other arithmetic: 4.55 us -> 2.26 us
  matrix products: 13.9 us -> 16.1 us
  starting transfers between devices: 10.9 us -> 13 us
    all_gather x1 -> x0, waiting for transfers between devices: 22.1 us -> none  [on_device(): every = lax.all_gather(panels, 'row', axis=1, tiled=True)]
    all_gather x1, blocking collectives: 7.2 us -> 21.9 us  [on_device(): small = lax.all_gather(small, 'row', axis=1, tiled=True)]
    all_to_all x1, waiting for transfers between devices: 60.8 us -> 52.6 us  [on_device(): moved = lax.all_to_all(tiles, 'col', 0, 0, tiled=True)]
    ppermute x0 -> x3, waiting for transfers between devices: none -> 7.84 us  [the longest x2 7.84 us: on_device(): earlier.append(lax.ppermute(earlier[-1], 'row', up))]
    unnamed x22 -> x48, local copies, waits for them, and re-layouts: 0.06 us -> 3.47 us
    dot_general x19, matrix products: 13.9 us -> 16.1 us  [mm(): return jnp.einsum(spec, *operands, precision=precision)]
    ppermute x0 -> x3, starting transfers between devices: none -> 2.15 us  [the longest x1 1.74 us: on_device(): later.append(lax.ppermute(later[-1], 'row', down))]
  transfers between devices with their start and end apart: 3 -> 5, of which waited for: 3 -> 3; matrix products, arithmetic and copies ran while one was open for 2% -> 7% of each run, Pallas kernels for 0% -> 0%
where the time goes in v1:
time: 133 us; the launch traced here: 132 us
  waiting for transfers between devices  65.8 us (49%)
  blocking collectives  21.9 us (16%)
  matrix products  16.1 us (12%)
  starting transfers between devices  13 us (10%)
  local copies, waits for them, and re-layouts  12.3 us (9%)
  other arithmetic  2.26 us (2%)
    all_to_all x1, waiting for transfers between devices, on_device(): moved = lax.all_to_all(tiles, 'col', 0, 0, tiled=True)  52.6 us
    all_gather x1, blocking collectives, on_device(): small = lax.all_gather(small, 'row', axis=1, tiled=True)  21.9 us
    dot_general x19, matrix products, mm(): return jnp.einsum(spec, *operands, precision=precision)  16.1 us
    ppermute x2, waiting for transfers between devices, on_device(): earlier.append(lax.ppermute(earlier[-1], 'row', up))  7.84 us
    all_to_all x1, starting transfers between devices, on_device(): moved = lax.all_to_all(tiles, 'col', 0, 0, tiled=True)  7.4 us
    all_to_all x1, waiting for transfers between devices, on_device(): parts = lax.all_to_all(parts, 'row', 1, 1, tiled=True)  5.36 us
    reshape x2, local copies, waits for them, and re-layouts, on_device(): local_tiles = ainv_top.reshape(tile_rows, width, tile_cols, width)  4.76 us
    unnamed x48, local copies, waits for them, and re-layouts  3.47 us
  transfers between devices with their start and end apart: 5, of which 3 were waited for; matrix products, arithmetic and copies ran while one was open for 7% of the time, Pallas kernels for 0%

profile of v1, /device:TPU:0, one launch (start us, length us, event | category | flops | bytes accessed | tf_op | source)
XLA Modules:
  0.0 132.4 jit_solution(9494493006125588796)
XLA Ops:
  0.6 2.9 %reshape.58 = f32[8,128,4,128]{3,2,1,0:T(4,128)} reshape(f32[1024,512]{1,0:T(8,128)} %param.9) | data formatting | bytes 4194304 | tf_op jit(solution)/shard_map/reshape | solution.py:28
  3.5 1.9 %copy.49 = f32[8,128,4,128]{3,1,2,0:T(8,128)S(1)} copy(f32[8,128,4,128]{3,2,1,0:T(4,128)} %reshape.58) | data formatting | bytes 4194304 | tf_op jit(solution)/shard_map/reshape | solution.py:28
  5.8 2.9 %gather_fusion = f32[64,128,128]{2,1,0:T(8,128)} fusion(f32[8,128,4,128]{3,1,2,0:T(8,128)S(1)} %copy.49, s32[64]{0:T(128)S(1)} %reshape.36), kind=kCustom, calls=%fused_computation | custom fusion | bytes 8389120 | tf_op jit(solution)/shard_map/gather | solution.py:33
  8.7 7.4 %all-to-all-start = ((f32[8,4,2,128,128]{4,3,2,1,0:T(8,128)}), f32[8,4,2,128,128]{4,3,2,1,0:T(8,128)}, u32[]{:S(2)}, u32[]{:S(2)}) async-start(f32[8,4,2,128,128]{4,3,2,1,0:T(8,128)} %bitcast.131), calls=%async_computation | async-start | bytes 8388608 | tf_op jit(solution)/shard_map/all_to_all | solution.py:51
  16.1 0.7 constant_dynamic-update-slice_fusion.1
  16.8 0.8 constant_dynamic-update-slice_fusion
  17.6 1.7 %collective-permute-start.2 = (f32[3,4,128,128]{3,2,1,0:T(8,128)}, f32[3,4,128,128]{3,2,1,0:T(8,128)S(1)}, u32[]{:S(2)}, u32[]{:S(2)}) collective-permute-start(f32[3,4,128,128]{3,2,1,0:T(8,128)} %constant_dynamic-update-slice_fusion), channel_id=1, source_target_pairs={{0,24},{8,0},{16,8},{24,16},{1,25},{9,1},{17,9},{25,17},{2,26},{10... | collective-permute-start | bytes 2359304 | tf_op jit(solution)/shard_map/ppermute | solution.py:48
  19.5 21.9 %all_gather.3 = f32[8,128,128]{2,1,0:T(8,128)S(1)} all-gather(f32[8,32,128]{2,1,0:T(8,128)S(1)} %constant_dynamic-update-slice_fusion.12), channel_id=1, replica_groups=mesh['row'=4,'col'=8] {'row'}, dimensions={1}, use_global_device_ids=true | all-gather | bytes 655360 | tf_op jit(solution)/shard_map/all_gather | solution.py:35
  41.6 0.3 convolution_bitcast_fusion.2
  42.2 0.4 collective-permute-start.1
  42.8 0.9 fusion.16
  43.8 0.9 fusion.24
  44.7 1.2 convolution_bitcast_fusion.1
  45.9 7.8 %collective-permute-done.1 = f32[3,4,128,128]{3,2,1,0:T(8,128)} collective-permute-done((f32[3,4,128,128]{3,2,1,0:T(8,128)S(1)}, f32[3,4,128,128]{3,2,1,0:T(8,128)}, u32[]{:S(2)}, u32[]{:S(2)}) %collective-permute-start.1) | collective-permute-done | bytes 786464 | tf_op jit(solution)/shard_map/ppermute | solution.py:46
  53.7 1.2 constant_dynamic-update-slice_fusion.11
  55.1 1.2 constant_dynamic-update-slice_fusion.6
  56.8 52.6 %all-to-all-done = f32[8,4,2,128,128]{4,3,2,1,0:T(8,128)} async-done(((f32[8,4,2,128,128]{4,3,2,1,0:T(8,128)}), f32[8,4,2,128,128]{4,3,2,1,0:T(8,128)}, u32[]{:S(2)}, u32[]{:S(2)}) %all-to-all-start) | async-done | bytes 4194336 | tf_op jit(solution)/shard_map/all_to_all | solution.py:51
  109.4 7.0 %fusion.3 = f32[3,4,128,128]{2,3,1,0:T(8,128)S(1)} fusion(f32[3,8,2,128,128,1]{4,3,2,1,5,0:T(8,128)S(1)} %bitcast.132, f32[8,4,2,128,128]{4,3,2,1,0:T(8,128)} %all-to-all-done), kind=kOutput, calls=%fused_computation.4 | convolution fusion | flops 2415919104 | bytes 8126464 | tf_op jit(solution)/shard_map/cjkab,nckbd->njad/dot_general | solution.py:11
  116.4 0.4 convolution_negate_fusion.1
  116.8 0.4 convolution_bitcast_fusion
  117.3 0.3 fusion.44
  117.5 0.4 fusion.10
  117.9 0.6 convolution_negate_fusion
  118.6 0.4 convolution_bitcast_fusion.3
  119.2 0.3 convolution_subtract_fusion
  119.5 0.8 pad_maximum_fusion
  120.2 3.5 %all-to-all-start.1 = ((f32[5,4,32,128]{3,2,0,1:T(8,128)}), f32[5,4,32,128]{3,2,0,1:T(8,128)S(1)}, u32[]{:S(2)}, u32[]{:S(2)}) async-start(f32[5,4,32,128]{3,2,0,1:T(8,128)} %pad_maximum_fusion), calls=%async_computation.1 | async-start | bytes 655360 | tf_op jit(solution)/shard_map/all_to_all | solution.py:67
  123.9 1.1 fusion.18
  125.0 5.4 %all-to-all-done.1 = f32[5,4,32,128]{3,2,0,1:T(8,128)S(1)} async-done(((f32[5,4,32,128]{3,2,0,1:T(8,128)}), f32[5,4,32,128]{3,2,0,1:T(8,128)S(1)}, u32[]{:S(2)}, u32[]{:S(2)}) %all-to-all-start.1) | async-done | bytes 327712 | tf_op jit(solution)/shard_map/all_to_all | solution.py:67
  130.4 0.6 fusion.38
  131.0 0.8 fusion.8
  131.8 0.6 slice_add_fusion.2
  (61 shorter events, 2.1 us)
Async XLA Ops:
  0.6 4.8 %copy-start.16 = (s32[8,16]{1,0:T(8,128)S(1)}, s32[8,16]{1,0:T(8,128)}, u32[]{:S(2)}) copy-start(s32[8,16]{1,0:T(8,128)} %param.10) | copy-start | bytes 1540
  8.7 7.4 %copy-start.5 = (f32[1,4,128,128]{3,2,1,0:T(8,128)S(1)}, f32[1,4,128,128]{3,2,1,0:T(8,128)}, u32[]{:S(2)}) copy-start(f32[1,4,128,128]{3,2,1,0:T(8,128)} %param.11) | copy-start | bytes 786436
  8.7 8.2 %copy-start.2 = (f32[2,4,128,128]{3,2,1,0:T(8,128)S(1)}, f32[2,4,128,128]{3,2,1,0:T(8,128)}, u32[]{:S(2)}) copy-start(f32[2,4,128,128]{3,2,1,0:T(8,128)} %param.14) | copy-start | bytes 1572868
  8.7 10.7 %copy-start.14 = (f32[1,32,128]{2,1,0:T(8,128)S(1)}, f32[1,32,128]{2,1,0:T(8,128)}, u32[]{:S(2)}) copy-start(f32[1,32,128]{2,1,0:T(8,128)} %param.12) | copy-start | bytes 49156
  8.7 10.7 %copy-start.15 = (f32[1,32,128]{2,1,0:T(8,128)S(1)}, f32[1,32,128]{2,1,0:T(8,128)}, u32[]{:S(2)}) copy-start(f32[1,32,128]{2,1,0:T(8,128)} %param.13) | copy-start | bytes 49156
  8.7 10.7 %copy-start.11 = (f32[2,32,128]{2,1,0:T(8,128)S(1)}, f32[2,32,128]{2,1,0:T(8,128)}, u32[]{:S(2)}) copy-start(f32[2,32,128]{2,1,0:T(8,128)} %param.15) | copy-start | bytes 98308
  8.7 10.8 %copy-start.12 = (f32[2,32,128]{2,1,0:T(8,128)S(1)}, f32[2,32,128]{2,1,0:T(8,128)}, u32[]{:S(2)}) copy-start(f32[2,32,128]{2,1,0:T(8,128)} %param.16) | copy-start | bytes 98308
  8.7 10.8 %copy-start.13 = (f32[2,32,128]{2,1,0:T(8,128)S(1)}, f32[2,32,128]{2,1,0:T(8,128)}, u32[]{:S(2)}) copy-start(f32[2,32,128]{2,1,0:T(8,128)} %param.17) | copy-start | bytes 98308
  8.7 100.7 %all-to-all-start = ((f32[8,4,2,128,128]{4,3,2,1,0:T(8,128)}), f32[8,4,2,128,128]{4,3,2,1,0:T(8,128)}, u32[]{:S(2)}, u32[]{:S(2)}) async-start(f32[8,4,2,128,128]{4,3,2,1,0:T(8,128)} %bitcast.131), calls=%async_computation | async-start | bytes 8388608 | tf_op jit(solution)/shard_map/all_to_all | solution.py:51
  17.6 24.5 %collective-permute-start = (f32[3,4,128,128]{3,2,1,0:T(8,128)}, f32[3,4,128,128]{3,2,1,0:T(8,128)S(1)}, u32[]{:S(2)}, u32[]{:S(2)}) collective-permute-start(f32[3,4,128,128]{3,2,1,0:T(8,128)} %constant_dynamic-update-slice_fusion), channel_id=1, source_target_pairs={{0,8},{8,16},{16,24},{24,0},{1,9},{9,17},{17,25},{25,1},{2,10},{10... | collective-permute-start | bytes 2359304 | tf_op jit(solution)/shard_map/ppermute | solution.py:46
  17.6 37.4 %collective-permute-start.2 = (f32[3,4,128,128]{3,2,1,0:T(8,128)}, f32[3,4,128,128]{3,2,1,0:T(8,128)S(1)}, u32[]{:S(2)}, u32[]{:S(2)}) collective-permute-start(f32[3,4,128,128]{3,2,1,0:T(8,128)} %constant_dynamic-update-slice_fusion), channel_id=1, source_target_pairs={{0,24},{8,0},{16,8},{24,16},{1,25},{9,1},{17,9},{25,17},{2,26},{10... | collective-permute-start | bytes 2359304 | tf_op jit(solution)/shard_map/ppermute | solution.py:48
  41.4 15.0 %copy-start = (f32[8,128,128]{2,1,0:T(8,128)}, f32[8,128,128]{2,1,0:T(8,128)S(1)}, u32[]{:S(2)}) copy-start(f32[8,128,128]{2,1,0:T(8,128)S(1)} %all_gather.3) | copy-start | bytes 1572868
  42.2 11.6 %collective-permute-start.1 = (f32[3,4,128,128]{3,2,1,0:T(8,128)S(1)}, f32[3,4,128,128]{3,2,1,0:T(8,128)}, u32[]{:S(2)}, u32[]{:S(2)}) collective-permute-start(f32[3,4,128,128]{3,2,1,0:T(8,128)S(1)} %collective-permute-done), channel_id=1, source_target_pairs={{0,8},{8,16},{16,24},{24,0},{1,9},{9,17},{17,25},{25,1},{2,10},{10... | collective-permute-start | bytes 2359304 | tf_op jit(solution)/shard_map/ppermute | solution.py:46
  42.8 13.7 %copy-start.9 = (f32[128,128]{1,0:T(8,128)}, f32[128,128]{1,0:T(8,128)S(1)}, u32[]{:S(2)}) copy-start(f32[128,128]{1,0:T(8,128)S(1)} %fusion.29) | copy-start | bytes 196612
  109.4 7.0 %copy-start.1 = (f32[8,128,128]{2,1,0:T(8,128)S(1)}, f32[8,128,128]{2,1,0:T(8,128)}, u32[]{:S(2)}) copy-start(f32[8,128,128]{2,1,0:T(8,128)} %copy-done) | copy-start | bytes 1572868
  109.4 8.1 %copy-start.3 = (f32[2,4,128,128]{2,3,1,0:T(8,128)S(1)}, f32[2,4,128,128]{2,3,1,0:T(8,128)}, u32[]{:S(2)}) copy-start(f32[2,4,128,128]{2,3,1,0:T(8,128)} %convolution_bitcast_fusion.1) | copy-start | bytes 1572868
  116.4 7.3 %copy-start.7 = (f32[128,2,128]{0,2,1:T(8,128)S(1)}, f32[128,2,128]{0,2,1:T(8,128)}, u32[]{:S(2)}) copy-start(f32[128,2,128]{0,2,1:T(8,128)} %fusion.24) | copy-start | bytes 393220
  116.4 7.5 %copy-start.8 = (f32[2,128,128]{1,2,0:T(8,128)S(1)}, f32[2,128,128]{1,2,0:T(8,128)}, u32[]{:S(2)}) copy-start(f32[2,128,128]{1,2,0:T(8,128)} %fusion.16) | copy-start | bytes 393220
  116.4 14.0 %copy-start.10 = (f32[128,128]{1,0:T(8,128)S(1)}, f32[128,128]{1,0:T(8,128)}, u32[]{:S(2)}) copy-start(f32[128,128]{1,0:T(8,128)} %copy-done.9) | copy-start | bytes 196612
  116.8 15.6 %copy-start.4 = (f32[4,128,128]{2,1,0:T(8,128)}, f32[4,128,128]{2,1,0:T(8,128)S(1)}, u32[]{:S(2)}) copy-start(f32[4,128,128]{2,1,0:T(8,128)S(1)} %convolution_negate_fusion.1) | copy-start | bytes 786436
  118.6 13.9 %copy-start.6 = (f32[2,4,128,128]{3,2,1,0:T(8,128)}, f32[2,4,128,128]{3,2,1,0:T(8,128)S(1)}, u32[]{:S(2)}) copy-start(f32[2,4,128,128]{3,2,1,0:T(8,128)S(1)} %convolution_negate_fusion) | copy-start | bytes 1572868
  120.2 10.2 %all-to-all-start.1 = ((f32[5,4,32,128]{3,2,0,1:T(8,128)}), f32[5,4,32,128]{3,2,0,1:T(8,128)S(1)}, u32[]{:S(2)}, u32[]{:S(2)}) async-start(f32[5,4,32,128]{3,2,0,1:T(8,128)} %pad_maximum_fusion), calls=%async_computation.1 | async-start | bytes 655360 | tf_op jit(solution)/shard_map/all_to_all | solution.py:67
